TPU v7x, 32 devices: a whole 2x2x4 slice. The times are simulated.
32 devices in a mesh: dp: 4 (over y, x), expert: 8 (over z, core).
Axes of the slice: x: 2, y: 2, z: 4, core: 2. Of those that a mesh axis runs over, the one named last changes fastest.
Arguments:
- tokens: bfloat16 [4096, 2048], P(('dp', 'expert')), may hold values from -6 to 6
- expert_ids: int32 [4096, 4], P(('dp', 'expert')), may hold values from 0 to 7, all different within a row; in each aligned block of 128 rows (0 to 127, 128 to 255, ...) at most 80 rows name the same one
- probs: float32 [4096, 4], P(('dp', 'expert')), may hold values from 0.2 to 1
- trade: int32 [4], replicated, may hold values from 0 to 1, as said below
- gate_weight: bfloat16 [8, 2048, 768], P('expert'), may hold values from -0.125 to 0.125
- up_weight: bfloat16 [8, 2048, 768], P('expert'), may hold values from -0.125 to 0.125
- down_weight: bfloat16 [8, 768, 2048], P('expert'), may hold values from -0.21875 to 0.21875
- out_grad: bfloat16 [4096, 2048], P(('dp', 'expert')), may hold values from -0.29882812 to 0.29882812
Outputs:
- combined: bfloat16 [4096, 2048], P(('dp', 'expert'))
- gate_grad: bfloat16 [8, 2048, 768], P('expert', 'dp')
- up_grad: bfloat16 [8, 2048, 768], P('expert', 'dp')
- down_grad: bfloat16 [8, 768, 2048], P('expert', None, 'dp')
Inputs may be any that keep to these rules, and one draw needn't show every extreme that they name: `trade`: index k below 4 pairs expert index k with k + 4; at least one pair trades and at least one does not. `expert_ids`: each row names 4 different experts. Within the 128 rows of one device no expert is named by more than 80 rows, a bound that some block reaches.
All inputs are finite; a program needn't handle non-finite values.
Results may differ from a plain program's by a relative error of at most 0.0095.
Values may be sent and summed in bfloat16 or wider, within the bound.
A program may use at most 128 MiB of HBM per device.

v0:
```python
import functools
import jax
import jax.numpy as jnp
from jax import lax
from jax.experimental import pallas as pl
from jax.experimental.pallas import tpu as pltpu
from jax.sharding import PartitionSpec as P


def sparse_local(tokens, expert_ids, probs, trade, gate_weight, up_weight, down_weight, out_grad):
    tok_count, model_width = tokens.shape
    top_count = expert_ids.shape[1]
    hidden_width = gate_weight.shape[2]
    experts = lax.axis_size("expert")
    capacity = 5 * tok_count * top_count // (4 * experts)
    halfway = experts // 2
    chosen = expert_ids.reshape(-1)
    numbers = jnp.arange(experts, dtype=jnp.int32)
    onehot = (chosen[:, None] == numbers[None, :]).astype(jnp.int32)
    earlier = jnp.cumsum(onehot, axis=0) - onehot
    slots = chosen * capacity + jnp.sum(earlier * onehot, axis=1)
    owners = jnp.where(trade[numbers % halfway] == 1, jnp.bitwise_xor(numbers, halfway), numbers)
    pair_tokens = jnp.arange(chosen.shape[0], dtype=jnp.int32) // top_count
    send_rows = (
        jnp.zeros((experts * capacity, model_width), jnp.bfloat16)
        .at[slots]
        .set(tokens[pair_tokens])
    )
    send_rows = send_rows.reshape(experts, capacity, model_width)
    out_pairs = (probs[:, :, None] * out_grad[:, None, :].astype(jnp.float32)).astype(jnp.bfloat16)
    send_grads = (
        jnp.zeros((experts * capacity, model_width), jnp.bfloat16)
        .at[slots]
        .set(out_pairs.reshape(-1, model_width))
    )
    send_grads = send_grads.reshape(experts, capacity, model_width)
    send_rows = send_rows[owners]
    send_grads = send_grads[owners]
    w_gate = gate_weight[0]
    w_up = up_weight[0]
    w_down = down_weight[0]
    arrived = lax.all_to_all(send_rows, "expert", split_axis=0, concat_axis=0, tiled=True)
    lead = arrived.shape[:2]
    flat_rows = arrived.reshape(-1, model_width)
    gate_act = jnp.dot(flat_rows, w_gate, preferred_element_type=jnp.float32)
    up_act = jnp.dot(flat_rows, w_up, preferred_element_type=jnp.float32)
    forward_hidden = (gate_act * jax.nn.sigmoid(gate_act) * up_act).astype(jnp.bfloat16)
    expert_out = jnp.dot(forward_hidden, w_down, preferred_element_type=jnp.float32).astype(
        jnp.bfloat16
    )
    arrived, expert_out, hidden, gate_act, up_act = (
        arrived,
        expert_out.reshape(lead + (model_width,)),
        forward_hidden.reshape(lead + (hidden_width,)),
        gate_act.reshape(lead + (hidden_width,)),
        up_act.reshape(lead + (hidden_width,)),
    )
    returned = lax.all_to_all(expert_out, "expert", split_axis=0, concat_axis=0, tiled=True)
    out_rows = lax.all_to_all(send_grads, "expert", split_axis=0, concat_axis=0, tiled=True)
    returned = returned[owners]
    picked = returned.reshape(-1, model_width)[slots].reshape(tok_count, top_count, model_width)
    combined = jnp.sum(probs[:, :, None] * picked.astype(jnp.float32), axis=1).astype(jnp.bfloat16)
    expert_rows = arrived.reshape(-1, model_width)
    out_rows = out_rows.reshape(-1, model_width)
    hidden = hidden.reshape(-1, hidden_width)
    gate_act = gate_act.reshape(-1, hidden_width)
    up_act = up_act.reshape(-1, hidden_width)
    hidden_grad = lax.dot_general(
        out_rows, w_down, (((1,), (1,)), ((), ())), preferred_element_type=jnp.float32
    )
    sigma = jax.nn.sigmoid(gate_act)
    gate_back = (hidden_grad * up_act * (sigma * (1.0 + gate_act * (1.0 - sigma)))).astype(
        jnp.bfloat16
    )
    up_back = (hidden_grad * (gate_act * sigma)).astype(jnp.bfloat16)
    both_back = jnp.concatenate([gate_back, up_back], axis=1)
    first = lax.dot_general(
        expert_rows, both_back, (((0,), (0,)), ((), ())), preferred_element_type=jnp.float32
    )
    second = lax.dot_general(
        out_rows, hidden, (((0,), (0,)), ((), ())), preferred_element_type=jnp.float32
    )
    summed = lax.psum_scatter(
        jnp.concatenate([first, second], axis=1).astype(jnp.bfloat16),
        "dp",
        scatter_dimension=0,
        tiled=True,
    )
    gate_part = summed[:, :hidden_width]
    up_part = summed[:, hidden_width : 2 * hidden_width]
    down_part = summed[:, 2 * hidden_width :].T
    return (combined, gate_part[None], up_part[None], down_part[None])


def layer_kernel(
    tokens, grads, weights, wg_hbm, wu_hbm, wd_hbm, combined, gate_out, up_out, down_out,
    rows, cots, wts, wg, wu, wd, wcol, hidden, back, acc, pairs, part, sib_part, far_part,
    gu, dn, gu_x, gu_y, dn_x, dn_y, gu_two, dn_two,
    load_sem, tok_send, tok_sib, tok_recv, cot_send, cot_sib, cot_recv, wt_send, wt_recv,
    part_sib, part_sib_recv, part_send, part_recv, red_send, red_recv,
):
    f32 = jnp.float32
    bf16 = jnp.bfloat16
    experts = lax.axis_size("expert")
    chips = experts // 2
    last = chips - 1
    replicas = lax.axis_size("dp")
    count, width = tokens.shape
    share = width // replicas
    ff = wg.shape[1]
    me = lax.axis_index("expert")
    z = me // 2
    c = me % 2
    d = lax.axis_index("dp")
    dx = (d // 2) * 2 + (1 - d % 2)
    dy = (1 - d // 2) * 2 + d % 2
    dd = 3 - d
    upper = z // (chips // 2)
    zm = z * (1 - upper) + (last - z) * upper
    sibling = z * 2 + (1 - c)
    inner = zm == 1

    def at_chip(m):
        return m * (1 - upper) + (last - m) * upper

    def other(q):
        return at_chip(jnp.where(q == 0, zm, jnp.where(q == 1, 1 - zm, q)))

    def source(q):
        m = jnp.where(jnp.logical_and(inner, q >= 2), last + 2 - q, q)
        return at_chip(jnp.where(q == 0, zm, jnp.where(q == 1, 1 - zm, m)))

    def owner_of(p):
        return jnp.where(p == 0, dd, jnp.where(p == 1, dx, jnp.where(p == 2, dy, d)))

    def lanes(p):
        return pl.ds(pl.multiple_of(owner_of(p) * share, share), share)

    def remote(src, dst, ssem, rsem, axis, to):
        return pltpu.make_async_remote_copy(
            src_ref=src, dst_ref=dst, send_sem=ssem, recv_sem=rsem,
            device_id={axis: to}, device_id_type=pl.DeviceIdType.MESH,
        )

    loads = [
        pltpu.make_async_copy(wg_hbm, wg, load_sem.at[0]),
        pltpu.make_async_copy(wu_hbm, wu, load_sem.at[1]),
        pltpu.make_async_copy(wd_hbm, wd, load_sem.at[2]),
        pltpu.make_async_copy(tokens, rows.at[me], load_sem.at[3]),
        pltpu.make_async_copy(weights, wts.at[me], load_sem.at[4]),
    ]
    loads[3].start()
    loads[4].start()

    def cot_load(p):
        return pltpu.make_async_copy(grads.at[:, lanes(p)], cots.at[p, me], load_sem.at[5 + p])

    for load in loads[:3]:
        load.start()
    for p in range(replicas):
        cot_load(p).start()

    barrier = pltpu.get_barrier_semaphore()
    for r in range(1, experts):
        pl.semaphore_signal(
            barrier, inc=1, device_id={"expert": (me + r) % experts},
            device_id_type=pl.DeviceIdType.MESH,
        )
    for to in (dx, dy):
        pl.semaphore_signal(
            barrier, inc=1, device_id={"dp": to}, device_id_type=pl.DeviceIdType.MESH
        )
    pl.semaphore_wait(barrier, experts + 1)

    def tok_copy(q):
        to = other(q) * 2 + c
        return remote(tokens, rows.at[me], tok_send.at[q], tok_recv.at[me], "expert", to)

    def cot_copy(p, q):
        to = other(q) * 2 + c
        return remote(
            grads.at[:, lanes(p)], cots.at[p, me], cot_send.at[p, q], cot_recv.at[p, me],
            "expert", to,
        )

    def each_target(fn):
        for q in (2, 1) + tuple(range(3, chips)):
            if q < last:
                fn(q)
            else:
                pl.when(inner)(functools.partial(fn, q))

    def wt_copy(r):
        return remote(
            weights, wts.at[me], wt_send.at[r], wt_recv.at[me], "expert", (me + r) % experts
        )

    for r in range(1, experts):
        wt_copy(r).start()
    each_target(lambda q: tok_copy(q).start())

    end = at_chip(0) * 2 + c

    def tok_from(slot):
        return remote(rows.at[slot], rows.at[slot], tok_send.at[0], tok_recv.at[slot], "expert", end)

    def tok_to_sib(zp):
        slot = zp * 2 + c
        return remote(
            rows.at[slot], rows.at[slot], tok_sib.at[zp], tok_recv.at[slot], "expert", sibling
        )

    def cot_from(p, slot):
        ref = cots.at[p, slot]
        return remote(ref, ref, cot_send.at[p, 0], cot_recv.at[p, slot], "expert", end)

    def cot_to_sib(p, zp):
        slot = zp * 2 + c
        ref = cots.at[p, slot]
        return remote(ref, ref, cot_sib.at[p, zp], cot_recv.at[p, slot], "expert", sibling)

    def part_to_sib(zp):
        return remote(
            part.at[zp * 2 + (1 - c)], sib_part.at[zp], part_sib.at[zp], part_sib_recv.at[zp],
            "expert", sibling,
        )

    loads[4].wait()
    for r in range(1, experts):
        slot = (me + r) % experts
        remote(weights, wts.at[slot], wt_send.at[r], wt_recv.at[slot], "expert", slot).wait_recv()
    eye = lax.broadcasted_iota(jnp.int32, (count, count), 0) == lax.broadcasted_iota(
        jnp.int32, (count, count), 1
    )
    for slot in range(experts):
        row = jnp.broadcast_to(wts[slot, pl.ds(me, 1), :], (count, count))
        column = jnp.sum(jnp.where(eye, row, 0.0), axis=1, keepdims=True)
        wcol[pl.ds(slot * count, count), :] = jnp.broadcast_to(column, (count, wcol.shape[1]))

    pair = 2 * count

    @pl.loop(0, chips)
    def _(q):
        zp = source(q)

        @pl.when(q == last)
        def _():
            for p in range(2):
                each_target(lambda q: cot_copy(p, q).start())

        @pl.when(q == 0)
        def _():
            loads[3].wait()

        @pl.when(q > 0)
        def _():
            tok_from(zp * 2 + c).wait_recv()

        @pl.when(jnp.logical_and(inner, q == last - 1))
        def _():
            tok_from(zp * 2 + c).start()

        tok_to_sib(zp).start()

        @pl.when(q == 0)
        def _():
            for load in loads[:3]:
                load.wait()

        tok_from(zp * 2 + (1 - c)).wait_recv()
        where = pl.ds(pl.multiple_of(zp * pair, pair), pair)
        x = rows[pl.ds(zp * 2, 2)].reshape(pair, width)
        tile = ff // 3

        @pl.loop(0, 3)
        def _(n):
            cols = pl.ds(pl.multiple_of(n * tile, tile), tile)
            g = jnp.dot(x, wg[:, cols], preferred_element_type=f32)
            u = jnp.dot(x, wu[:, cols], preferred_element_type=f32)
            sigma = jax.nn.sigmoid(g)
            silu = g * sigma
            hidden[where, cols] = (silu * u).astype(bf16)
            back[where, cols] = (u * (sigma * (1.0 + g * (1.0 - sigma)))).astype(bf16)
            back[where, pl.ds(pl.multiple_of(ff + n * tile, tile), tile)] = silu.astype(bf16)

        @pl.loop(0, replicas)
        def _(n):
            cols = pl.ds(pl.multiple_of(n * share, share), share)
            o = jnp.dot(hidden[where, :], wd[:, cols], preferred_element_type=f32)
            o = (o * wcol[where, 0:1]).astype(bf16)
            part[zp * 2, :, cols] = o[:count]
            part[zp * 2 + 1, :, cols] = o[count:]

        part_to_sib(zp).start()

    def part_copy(q):
        zp = other(q)
        return remote(
            part.at[zp * 2 + c], far_part.at[z], part_send.at[q], part_recv.at[z], "expert",
            zp * 2 + c,
        )

    half = share // 2
    fhalf = ff // 2

    def reduce_copy(step, wide):
        send, far = (gu, (gu_x, gu_y, gu_two)) if wide else (dn, (dn_x, dn_y, dn_two))
        h = half if wide else fhalf
        lo, hi = pl.ds(0, h), pl.ds(h, h)
        src, dst, axis_to = {
            0: (send.at[0, lo], far[0].at[0], dx),
            1: (send.at[0, hi], far[1].at[0], dy),
            2: (send.at[1, lo], far[0].at[1], dx),
            3: (send.at[2, hi], far[1].at[1], dy),
            4: (send.at[2, lo], far[2].at[0], dy),
            5: (send.at[1, hi], far[2].at[1], dx),
        }[step]
        k = step + 6 * int(wide)
        return remote(src, dst, red_send.at[k], red_recv.at[k], "dp", axis_to)

    def reduce_step(p, wide):
        send, far = (gu, (gu_x, gu_y)) if wide else (dn, (dn_x, dn_y))
        h = half if wide else fhalf
        lo, hi = pl.ds(0, h), pl.ds(h, h)

        @pl.when(p == 0)
        def _():
            reduce_copy(0, wide).start()
            reduce_copy(1, wide).start()

        @pl.when(p == 1)
        def _():
            reduce_copy(2, wide).start()

        @pl.when(p == 2)
        def _():
            reduce_copy(3, wide).start()

        @pl.when(p == (3 if wide else 2))
        def _():
            reduce_copy(0, wide).wait_recv()
            send[2, lo] = (send[2, lo].astype(f32) + far[0][0].astype(f32)).astype(bf16)
            reduce_copy(4, wide).start()
            reduce_copy(1, wide).wait_recv()
            send[1, hi] = (send[1, hi].astype(f32) + far[1][0].astype(f32)).astype(bf16)
            reduce_copy(5, wide).start()

    @pl.loop(0, replicas)
    def _(p):
        for q in range(chips):
            zp = source(q)
            if q == 0:
                cot_load(p).wait()
            else:
                cot_from(p, zp * 2 + c).wait_recv()
            if q == last - 1:

                @pl.when(inner)
                def _():
                    cot_from(p, zp * 2 + c).start()

            cot_to_sib(p, zp).start()

        @pl.when(p < replicas - 2)
        def _():
            each_target(lambda q: cot_copy(p + 2, q).start())

        @pl.when(p == replicas - 1)
        def _():
            for q in range(last, 0, -1):
                part_copy(q).start()

        for zp in range(chips):
            cot_from(p, zp * 2 + (1 - c)).wait_recv()
        for slot in range(experts):
            where = pl.ds(slot * count, count)
            pairs[where, :] = (wcol[where, 0:1] * cots[p, slot].astype(f32)).astype(bf16)
        tile = ff // 3

        @pl.loop(0, 3)
        def _(n):
            cols = pl.ds(pl.multiple_of(n * tile, tile), tile)
            dn[p, cols, :] = lax.dot_general(
                hidden[:, cols], pairs[...], (((0,), (0,)), ((), ())), preferred_element_type=f32
            ).astype(bf16)

        reduce_step(p, False)

        @pl.when(p == 0)
        def _():
            for zp in range(chips):
                remote(
                    part.at[zp * 2 + (1 - c)], sib_part.at[zp], part_sib.at[zp],
                    part_sib_recv.at[zp], "expert", sibling,
                ).wait_recv()
                part[zp * 2 + c] = (
                    part[zp * 2 + c].astype(f32) + sib_part[zp].astype(f32)
                ).astype(bf16)

        @pl.loop(0, 3)
        def _(n):
            cols = pl.ds(pl.multiple_of(n * tile, tile), tile)
            more = lax.dot_general(
                pairs[...], wd[cols, lanes(p)], (((1,), (1,)), ((), ())),
                preferred_element_type=f32,
            )
            acc[:, cols] = jnp.where(p == 0, more, acc[:, cols] + more)

    @pl.loop(0, experts)
    def _(n):
        where = pl.ds(pl.multiple_of(n * count, count), count)
        back[where, :ff] = (acc[where, :] * back[where, :ff].astype(f32)).astype(bf16)
        back[where, ff:] = (acc[where, :] * back[where, ff:].astype(f32)).astype(bf16)

    @pl.loop(0, replicas)
    def _(p):
        for h in range(2):
            cols = pl.ds(pl.multiple_of(owner_of(p) * share + h * half, half), half)
            lhs = rows[:, :, cols].reshape(experts * count, half)
            for n in range(2):
                gu[p, h * half:(h + 1) * half, n * ff:(n + 1) * ff] = lax.dot_general(
                    lhs, back[:, n * ff:(n + 1) * ff], (((0,), (0,)), ((), ())),
                    preferred_element_type=f32,
                ).astype(bf16)
        reduce_step(p, True)

    def finish(wide):
        for k in (2, 3, 4, 5):
            reduce_copy(k, wide).wait_recv()

    def total(own, one, two):
        return (own.astype(f32) + one.astype(f32) + two.astype(f32)).astype(bf16)

    finish(False)
    down_out[:fhalf] = total(dn[3, :fhalf], dn_x[1], dn_two[0])
    down_out[fhalf:] = total(dn[3, fhalf:], dn_y[1], dn_two[1])
    for q in range(1, chips):
        zp = other(q)
        remote(
            part.at[zp * 2 + c], far_part.at[zp], part_send.at[q], part_recv.at[zp], "expert",
            zp * 2 + c,
        ).wait_recv()
    mixed = part[me].astype(f32)
    for q in range(1, chips):
        mixed = mixed + far_part[other(q)].astype(f32)
    combined[...] = mixed.astype(bf16)
    finish(True)
    for n, out in ((0, gate_out), (1, up_out)):
        cols = slice(n * ff, (n + 1) * ff)
        out[:half] = total(gu[3, :half, cols], gu_x[1, :, cols], gu_two[0, :, cols])
        out[half:] = total(gu[3, half:, cols], gu_y[1, :, cols], gu_two[1, :, cols])

    each_target(lambda q: tok_copy(q).wait_send())
    for p in range(replicas):
        each_target(lambda q: cot_copy(p, q).wait_send())
    for r in range(1, experts):
        wt_copy(r).wait_send()
    for q in range(chips):
        zp = other(q)
        tok_to_sib(zp).wait_send()
        part_to_sib(zp).wait_send()
        for p in range(replicas):
            cot_to_sib(p, zp).wait_send()
        if q > 0:
            part_copy(q).wait_send()

    @pl.when(inner)
    def _():
        slot = source(last - 1) * 2 + c
        tok_from(slot).wait_send()
        for p in range(replicas):
            cot_from(p, slot).wait_send()

    for wide in (False, True):
        for k in range(6):
            reduce_copy(k, wide).wait_send()


def chain_local(tokens, expert_ids, probs, trade, gate_weight, up_weight, down_weight, out_grad):
    count, width = tokens.shape
    ff = gate_weight.shape[2]
    experts = lax.axis_size("expert")
    replicas = lax.axis_size("dp")
    chips = experts // 2
    share = width // replicas
    halfway = experts // 2
    numbers = jnp.arange(experts, dtype=jnp.int32)
    owners = jnp.where(
        jnp.concatenate([trade, trade]) == 1, jnp.bitwise_xor(numbers, halfway), numbers
    )
    weights = jnp.sum(
        jnp.where(expert_ids.T[None] == owners[:, None, None], probs.T[None], 0.0), axis=1
    )
    bf16, f32 = jnp.bfloat16, jnp.float32
    dma = pltpu.SemaphoreType.DMA
    total = experts * count
    hbm = pl.BlockSpec(memory_space=pl.ANY)
    vmem = pl.BlockSpec(memory_space=pltpu.VMEM)
    combined, gate, up, down = pl.pallas_call(
        layer_kernel,
        out_shape=(
            jax.ShapeDtypeStruct((count, width), bf16),
            jax.ShapeDtypeStruct((share, ff), bf16),
            jax.ShapeDtypeStruct((share, ff), bf16),
            jax.ShapeDtypeStruct((ff, share), bf16),
        ),
        in_specs=[hbm] * 6,
        out_specs=(vmem,) * 4,
        scratch_shapes=[
            pltpu.VMEM((experts, count, width), bf16),
            pltpu.VMEM((replicas, experts, count, share), bf16),
            pltpu.VMEM((experts, experts, count), f32),
            pltpu.VMEM((width, ff), bf16),
            pltpu.VMEM((width, ff), bf16),
            pltpu.VMEM((ff, width), bf16),
            pltpu.VMEM((total, count), f32),
            pltpu.VMEM((total, ff), bf16),
            pltpu.VMEM((total, 2 * ff), bf16),
            pltpu.VMEM((total, ff), f32),
            pltpu.VMEM((total, share), bf16),
            pltpu.VMEM((experts, count, width), bf16),
            pltpu.VMEM((chips, count, width), bf16),
            pltpu.VMEM((chips, count, width), bf16),
            pltpu.VMEM((replicas, share, 2 * ff), bf16),
            pltpu.VMEM((replicas, ff, share), bf16),
            pltpu.VMEM((2, share // 2, 2 * ff), bf16),
            pltpu.VMEM((2, share // 2, 2 * ff), bf16),
            pltpu.VMEM((2, ff // 2, share), bf16),
            pltpu.VMEM((2, ff // 2, share), bf16),
            pltpu.VMEM((2, share // 2, 2 * ff), bf16),
            pltpu.VMEM((2, ff // 2, share), bf16),
            dma((5 + replicas,)),
            dma((chips,)),
            dma((chips,)),
            dma((experts,)),
            dma((replicas, chips)),
            dma((replicas, chips)),
            dma((replicas, experts)),
            dma((experts,)),
            dma((experts,)),
            dma((chips,)),
            dma((chips,)),
            dma((chips,)),
            dma((chips,)),
            dma((12,)),
            dma((12,)),
        ],
        compiler_params=pltpu.CompilerParams(
            collective_id=0, has_side_effects=True, vmem_limit_bytes=67043328
        ),
    )(tokens, out_grad, weights, gate_weight[0], up_weight[0], down_weight[0])
    return combined, gate[None], up[None], down[None]


def local(tokens, expert_ids, *rest):
    experts, replicas = lax.axis_size("expert"), lax.axis_size("dp")
    capacity = 5 * tokens.shape[0] * expert_ids.shape[1] // (4 * experts)
    if tokens.shape[0] <= 2 * capacity and experts == 8 and replicas == 4:
        return chain_local(tokens, expert_ids, *rest)
    return sparse_local(tokens, expert_ids, *rest)


def solution(mesh):
    return jax.shard_map(
        local,
        mesh=mesh,
        in_specs=(
            P(("dp", "expert"), None),
            P(("dp", "expert"), None),
            P(("dp", "expert"), None),
            P(),
            P("expert", None, None),
            P("expert", None, None),
            P("expert", None, None),
            P(("dp", "expert"), None),
        ),
        out_specs=(
            P(("dp", "expert"), None),
            P("expert", "dp", None),
            P("expert", "dp", None),
            P("expert", None, "dp"),
        ),
        check_vma=False,
    )
```

profile of v0, /device:TPU:0, one launch (start us, length us, event | category | flops | bytes accessed | tf_op | source)
XLA Modules:
  0.0 172.9 jit_solution(15445759902657052885)
XLA Ops:
  0.6 0.8 compare_select_fusion
  1.4 1.4 select_reduce_fusion.weights
  2.8 164.2 %shard_map.111 = (bf16[128,2048]{1,0:T(8,128)(2,1)}, bf16[512,768]{1,0:T(8,128)(2,1)}, bf16[512,768]{1,0:T(8,128)(2,1)}, bf16[768,512]{1,0:T(8,128)(2,1)}) custom-call(bf16[128,2048]{1,0:T(8,128)(2,1)} %tokens.1, bf16[128,2048]{1,0:T(8,128)(2,1)} %grads.1, f32[8,128]{1,0:T(8,128)} %select_reduce_fusion.weights, bf16[2048,768]{1,0:T(8,128)(2,1)} %bitcast.8, ...), custom_call_target="tpu_custom_call" | custom-call | tf_op jit(solution)/shard_map/pallas_call | solution.py:499
  167.0 0.0 copy-start.1
  167.0 0.0 copy-start
  167.0 2.0 %copy.16 = bf16[128,2048]{1,0:T(8,128)(2,1)} copy(bf16[128,2048]{1,0:T(8,128)(2,1)} %get-tuple-element.16) | data formatting | bytes 1048576
  169.0 2.1 %copy.17 = bf16[1,512,768]{2,1,0:T(8,128)(2,1)} copy(bf16[1,512,768]{2,1,0:T(8,128)(2,1)} %bitcast.13) | data formatting | bytes 1572864
  171.1 0.0 copy-done.1
  171.1 0.9 copy.18
  172.0 0.0 copy-done
  172.0 0.9 copy.19
Async XLA Ops:
  167.0 4.1 %copy-start.1 = (bf16[512,768]{1,0:T(8,128)(2,1)S(1)}, bf16[512,768]{1,0:T(8,128)(2,1)}, u32[]{:S(2)}) copy-start(bf16[512,768]{1,0:T(8,128)(2,1)} %get-tuple-element.10) | copy-start | bytes 2359300
  167.0 5.0 %copy-start = (bf16[768,512]{1,0:T(8,128)(2,1)S(1)}, bf16[768,512]{1,0:T(8,128)(2,1)}, u32[]{:S(2)}) copy-start(bf16[768,512]{1,0:T(8,128)(2,1)} %get-tuple-element.11) | copy-start | bytes 2359300
where the time goes:
time: 173 us
  Pallas kernels  164 us (95%)
  local copies, waits for them, and re-layouts  5.83 us (3%)
  other arithmetic  2.17 us (1%)
    pallas_call x1, Pallas kernels, chain_local(): pl.pallas_call(layer_kernel, out_shape=(jax.ShapeDtypeStruct((count, widt...  164 us
    unnamed x8, local copies, waits for them, and re-layouts  5.83 us

commit v1 on v0

v1 whole, which is shorter than its diff:
```python
import functools
import jax
import jax.numpy as jnp
from jax import lax
from jax.experimental import pallas as pl
from jax.experimental.pallas import tpu as pltpu
from jax.sharding import PartitionSpec as P


def sparse_local(tokens, expert_ids, probs, trade, gate_weight, up_weight, down_weight, out_grad):
    tok_count, model_width = tokens.shape
    top_count = expert_ids.shape[1]
    hidden_width = gate_weight.shape[2]
    experts = lax.axis_size("expert")
    capacity = 5 * tok_count * top_count // (4 * experts)
    halfway = experts // 2
    chosen = expert_ids.reshape(-1)
    numbers = jnp.arange(experts, dtype=jnp.int32)
    onehot = (chosen[:, None] == numbers[None, :]).astype(jnp.int32)
    earlier = jnp.cumsum(onehot, axis=0) - onehot
    slots = chosen * capacity + jnp.sum(earlier * onehot, axis=1)
    owners = jnp.where(trade[numbers % halfway] == 1, jnp.bitwise_xor(numbers, halfway), numbers)
    pair_tokens = jnp.arange(chosen.shape[0], dtype=jnp.int32) // top_count
    send_rows = (
        jnp.zeros((experts * capacity, model_width), jnp.bfloat16)
        .at[slots]
        .set(tokens[pair_tokens])
    )
    send_rows = send_rows.reshape(experts, capacity, model_width)
    out_pairs = (probs[:, :, None] * out_grad[:, None, :].astype(jnp.float32)).astype(jnp.bfloat16)
    send_grads = (
        jnp.zeros((experts * capacity, model_width), jnp.bfloat16)
        .at[slots]
        .set(out_pairs.reshape(-1, model_width))
    )
    send_grads = send_grads.reshape(experts, capacity, model_width)
    send_rows = send_rows[owners]
    send_grads = send_grads[owners]
    w_gate = gate_weight[0]
    w_up = up_weight[0]
    w_down = down_weight[0]
    arrived = lax.all_to_all(send_rows, "expert", split_axis=0, concat_axis=0, tiled=True)
    lead = arrived.shape[:2]
    flat_rows = arrived.reshape(-1, model_width)
    gate_act = jnp.dot(flat_rows, w_gate, preferred_element_type=jnp.float32)
    up_act = jnp.dot(flat_rows, w_up, preferred_element_type=jnp.float32)
    forward_hidden = (gate_act * jax.nn.sigmoid(gate_act) * up_act).astype(jnp.bfloat16)
    expert_out = jnp.dot(forward_hidden, w_down, preferred_element_type=jnp.float32).astype(
        jnp.bfloat16
    )
    arrived, expert_out, hidden, gate_act, up_act = (
        arrived,
        expert_out.reshape(lead + (model_width,)),
        forward_hidden.reshape(lead + (hidden_width,)),
        gate_act.reshape(lead + (hidden_width,)),
        up_act.reshape(lead + (hidden_width,)),
    )
    returned = lax.all_to_all(expert_out, "expert", split_axis=0, concat_axis=0, tiled=True)
    out_rows = lax.all_to_all(send_grads, "expert", split_axis=0, concat_axis=0, tiled=True)
    returned = returned[owners]
    picked = returned.reshape(-1, model_width)[slots].reshape(tok_count, top_count, model_width)
    combined = jnp.sum(probs[:, :, None] * picked.astype(jnp.float32), axis=1).astype(jnp.bfloat16)
    expert_rows = arrived.reshape(-1, model_width)
    out_rows = out_rows.reshape(-1, model_width)
    hidden = hidden.reshape(-1, hidden_width)
    gate_act = gate_act.reshape(-1, hidden_width)
    up_act = up_act.reshape(-1, hidden_width)
    hidden_grad = lax.dot_general(
        out_rows, w_down, (((1,), (1,)), ((), ())), preferred_element_type=jnp.float32
    )
    sigma = jax.nn.sigmoid(gate_act)
    gate_back = (hidden_grad * up_act * (sigma * (1.0 + gate_act * (1.0 - sigma)))).astype(
        jnp.bfloat16
    )
    up_back = (hidden_grad * (gate_act * sigma)).astype(jnp.bfloat16)
    both_back = jnp.concatenate([gate_back, up_back], axis=1)
    first = lax.dot_general(
        expert_rows, both_back, (((0,), (0,)), ((), ())), preferred_element_type=jnp.float32
    )
    second = lax.dot_general(
        out_rows, hidden, (((0,), (0,)), ((), ())), preferred_element_type=jnp.float32
    )
    summed = lax.psum_scatter(
        jnp.concatenate([first, second], axis=1).astype(jnp.bfloat16),
        "dp",
        scatter_dimension=0,
        tiled=True,
    )
    gate_part = summed[:, :hidden_width]
    up_part = summed[:, hidden_width : 2 * hidden_width]
    down_part = summed[:, 2 * hidden_width :].T
    return (combined, gate_part[None], up_part[None], down_part[None])


def layer_kernel(
    tokens, grads, weights, wg_hbm, wu_hbm, wd_hbm, combined, gate_out, up_out, down_out,
    rows, cots, wts, wg, wu, wd, wcol, hidden, back, acc, pairs, part, sib_part, far_part,
    gu, gu_far, dn, dn_far,
    load_sem, out_sem, tok_send, tok_sib, tok_recv, cot_send, cot_sib, cot_recv, wt_send, wt_recv,
    part_sib, part_sib_recv, part_send, part_recv, gu_send, gu_recv, dn_send, dn_recv,
):
    f32 = jnp.float32
    bf16 = jnp.bfloat16
    experts = lax.axis_size("expert")
    chips = experts // 2
    last = chips - 1
    replicas = lax.axis_size("dp")
    count, width = tokens.shape
    share = width // replicas
    half = share // 2
    ff = wg.shape[1]
    pair = 2 * count
    me = lax.axis_index("expert")
    z = me // 2
    c = me % 2
    d = lax.axis_index("dp")
    dx = (d // 2) * 2 + (1 - d % 2)
    dy = (1 - d // 2) * 2 + d % 2
    dd = 3 - d
    upper = z // (chips // 2)
    zm = z * (1 - upper) + (last - z) * upper
    sibling = z * 2 + (1 - c)
    inner = zm == 1
    outer = zm == 0

    def at_chip(m):
        return m * (1 - upper) + (last - m) * upper

    def source(q):
        return at_chip(jnp.where(q == 0, zm, jnp.where(q == 1, 1 - zm, q)))

    def cols_of(s, side):
        to = jnp.where(side == 0, dx, dy)
        owner = jnp.where(s == 0, dd, jnp.where(s == 3, d, to))
        h = jnp.where(s == 2, 1 - side, side)
        return pl.ds(pl.multiple_of(owner * share + h * half, half), half)

    def remote(src, dst, ssem, rsem, axis, to):
        return pltpu.make_async_remote_copy(
            src_ref=src, dst_ref=dst, send_sem=ssem, recv_sem=rsem,
            device_id={axis: to}, device_id_type=pl.DeviceIdType.MESH,
        )

    loads = [
        pltpu.make_async_copy(wg_hbm, wg, load_sem.at[0]),
        pltpu.make_async_copy(wu_hbm, wu, load_sem.at[1]),
        pltpu.make_async_copy(wd_hbm, wd, load_sem.at[2]),
        pltpu.make_async_copy(tokens, rows.at[me], load_sem.at[3]),
        pltpu.make_async_copy(weights, wts.at[me], load_sem.at[4]),
    ]

    def cot_load(p, side):
        return pltpu.make_async_copy(
            grads.at[:, cols_of(p, side)], cots.at[p, me, :, pl.ds(side * half, half)],
            load_sem.at[5 + 2 * p + side],
        )

    loads[3].start()
    loads[4].start()
    for p in range(replicas):
        for side in range(2):
            cot_load(p, side).start()
    for load in loads[:3]:
        load.start()

    barrier = pltpu.get_barrier_semaphore()
    for r in range(1, experts):
        pl.semaphore_signal(
            barrier, inc=1, device_id={"expert": (me + r) % experts},
            device_id_type=pl.DeviceIdType.MESH,
        )
    for to in (dx, dy):
        pl.semaphore_signal(
            barrier, inc=1, device_id={"dp": to}, device_id_type=pl.DeviceIdType.MESH
        )
    pl.semaphore_wait(barrier, experts + 1)

    to_chip = (at_chip(0) * 2 + c, at_chip(zm + 1) * 2 + c)
    rhalf = count // 2

    def tok_own(way, h):
        part_rows = pl.ds(h * rhalf, rhalf)
        return remote(
            tokens.at[part_rows], rows.at[me, part_rows], tok_send.at[way, z, h],
            tok_recv.at[me, h], "expert", to_chip[way],
        )

    def tok_hop(way, zp, h):
        ref = rows.at[zp * 2 + c, pl.ds(h * rhalf, rhalf)]
        return remote(
            ref, ref, tok_send.at[way, zp, h], tok_recv.at[zp * 2 + c, h], "expert", to_chip[way]
        )

    def tok_to_sib(zp):
        ref = rows.at[zp * 2 + c]
        return remote(ref, ref, tok_sib.at[zp], tok_recv.at[zp * 2 + c, 0], "expert", sibling)

    def cot_hop(way, p, zp):
        ref = cots.at[p, zp * 2 + c]
        return remote(
            ref, ref, cot_send.at[way, p, zp], cot_recv.at[p, zp * 2 + c], "expert", to_chip[way]
        )

    def cot_to_sib(p, zp):
        ref = cots.at[p, zp * 2 + c]
        return remote(ref, ref, cot_sib.at[p, zp], cot_recv.at[p, zp * 2 + c], "expert", sibling)

    def wt_copy(r):
        return remote(
            weights, wts.at[me], wt_send.at[r], wt_recv.at[me], "expert", (me + r) % experts
        )

    def wt_from(slot):
        return remote(
            weights, wts.at[slot], wt_send.at[1], wt_recv.at[slot], "expert", sibling
        )

    own_to_sib = remote(
        tokens, rows.at[me], tok_sib.at[z], tok_recv.at[me, 0], "expert", sibling
    )

    for r in range(1, experts):
        wt_copy(r).start()
    own_to_sib.start()
    for h in range(2):
        tok_own(1, h).start()
        pl.when(inner)(tok_own(0, h).start)
    for p in range(replicas):
        for side in range(2):
            cot_load(p, side).wait()
        cot_to_sib(p, z).start()

        pl.when(outer)(cot_hop(1, p, z).start)

    def part_to_sib(zp):
        return remote(
            part.at[zp * 2 + (1 - c)], sib_part.at[zp], part_sib.at[zp], part_sib_recv.at[zp],
            "expert", sibling,
        )

    eye = lax.broadcasted_iota(jnp.int32, (count, count), 0) == lax.broadcasted_iota(
        jnp.int32, (count, count), 1
    )

    def weight_column(slot):
        row = jnp.broadcast_to(wts[slot, pl.ds(me, 1), :], (count, count))
        column = jnp.sum(jnp.where(eye, row, 0.0), axis=1, keepdims=True)
        wcol[pl.ds(pl.multiple_of(slot * count, count), count), :] = jnp.broadcast_to(
            column, (count, wcol.shape[1])
        )

    loads[3].wait()
    loads[4].wait()

    @pl.loop(0, chips)
    def _(q):
        zp = source(q)
        slot = zp * 2 + c

        @pl.when(jnp.logical_and(q > 0, jnp.logical_not(jnp.logical_and(inner, q == 2))))
        def _():
            @pl.when(jnp.logical_not(jnp.logical_and(inner, q == 3)))
            def _():
                tok_hop(0, zp, 0).wait_recv()

                @pl.when(inner)
                def _():
                    tok_hop(1, zp, 0).start()
                    tok_hop(0, at_chip(2), 0).wait_recv()
                    tok_hop(0, at_chip(2), 0).start()

            tok_hop(0, zp, 1).wait_recv()

            @pl.when(jnp.logical_and(inner, q == 1))
            def _():
                tok_hop(1, zp, 1).start()
                tok_hop(0, at_chip(2), 1).wait_recv()
                tok_hop(0, at_chip(2), 1).start()
                tok_to_sib(at_chip(2)).start()

            @pl.when(jnp.logical_and(inner, q == 3))
            def _():
                tok_hop(0, zp, 1).start()
                cot_hop(0, 0, z).start()

            tok_to_sib(zp).start()

        @pl.when(jnp.logical_and(inner, q == 2))
        def _():
            for p in range(replicas):
                cot_hop(1, p, z).start()
                cot_hop(1, p, at_chip(0)).wait_recv()
                cot_hop(1, p, at_chip(0)).start()
            tok_hop(0, at_chip(3), 0).wait_recv()
            tok_hop(0, at_chip(3), 0).start()

        @pl.when(q == 0)
        def _():
            wt_from(sibling).wait_recv()
            weight_column(me)
            weight_column(sibling)
            for load in loads[:3]:
                load.wait()

        @pl.when(q > 0)
        def _():
            for k in range(2):
                wt_from(zp * 2 + k).wait_recv()
                weight_column(zp * 2 + k)

        remote(
            rows.at[zp * 2 + 1 - c], rows.at[zp * 2 + 1 - c], tok_sib.at[zp],
            tok_recv.at[zp * 2 + 1 - c, 0], "expert", sibling,
        ).wait_recv()
        where = pl.ds(pl.multiple_of(zp * pair, pair), pair)
        x = rows[pl.ds(zp * 2, 2)].reshape(pair, width)
        tile = ff // 3

        @pl.loop(0, 3)
        def _(n):
            cols = pl.ds(pl.multiple_of(n * tile, tile), tile)
            g = jnp.dot(x, wg[:, cols], preferred_element_type=f32)
            u = jnp.dot(x, wu[:, cols], preferred_element_type=f32)
            sigma = jax.nn.sigmoid(g)
            silu = g * sigma
            hidden[where, cols] = (silu * u).astype(bf16)
            back[where, cols] = (u * (sigma * (1.0 + g * (1.0 - sigma)))).astype(bf16)
            back[where, pl.ds(pl.multiple_of(ff + n * tile, tile), tile)] = silu.astype(bf16)

        @pl.loop(0, replicas)
        def _(n):
            cols = pl.ds(pl.multiple_of(n * share, share), share)
            o = jnp.dot(hidden[where, :], wd[:, cols], preferred_element_type=f32)
            o = (o * wcol[where, 0:1]).astype(bf16)
            part[zp * 2, :, cols] = o[:count]
            part[zp * 2 + 1, :, cols] = o[count:]

        part_to_sib(zp).start()

    def part_copy(m):
        zp = at_chip(m)
        return remote(
            part.at[zp * 2 + c], far_part.at[z], part_send.at[m], part_recv.at[z], "expert",
            zp * 2 + c,
        )

    def dn_copy(s, side):
        return remote(
            dn.at[s, side], dn_far.at[side, s], dn_send.at[s, side], dn_recv.at[side, s], "dp",
            (dx, dy)[side],
        )

    def down_grad(p):
        for side in range(2):
            dn[p, side] = lax.dot_general(
                hidden[...], pairs[:, side * half:(side + 1) * half], (((0,), (0,)), ((), ())),
                preferred_element_type=f32,
            ).astype(bf16)

    def add(a, b):
        return (a.astype(f32) + b.astype(f32)).astype(bf16)

    @pl.loop(0, replicas)
    def _(p):
        def use(q):
            zp = source(q)
            other = zp * 2 + 1 - c
            remote(
                cots.at[p, other], cots.at[p, other], cot_sib.at[p, zp], cot_recv.at[p, other],
                "expert", sibling,
            ).wait_recv()
            where = pl.ds(pl.multiple_of(zp * pair, pair), pair)
            both = cots[p, pl.ds(zp * 2, 2)].reshape(pair, share)
            scaled = (wcol[where, 0:1] * both.astype(f32)).astype(bf16)
            pairs[where, :] = scaled
            more = lax.dot_general(
                scaled,
                jnp.concatenate([wd[:, cols_of(p, 0)], wd[:, cols_of(p, 1)]], axis=1),
                (((1,), (1,)), ((), ())), preferred_element_type=f32,
            )
            total = jnp.where(p == 0, more, acc[where, :] + more)
            acc[where, :] = total

            @pl.when(p == replicas - 1)
            def _():
                for n in range(2):
                    cols = slice(n * ff, (n + 1) * ff)
                    back[where, cols] = (acc[where, :] * back[where, cols].astype(f32)).astype(bf16)

        for q in range(chips):
            zp = source(q)
            if q == 1:
                pl.when(outer)(cot_hop(0, p, zp).wait_recv)
            elif q > 1:
                cot_hop(0, p, zp).wait_recv()
                pl.when(inner)(cot_hop(0, p, zp).start)
            if q > 0:
                cot_to_sib(p, zp).start()
            if q == last:

                @pl.when(jnp.logical_and(inner, p < replicas - 1))
                def _():
                    cot_hop(0, p + 1, z).start()

            if q > 0:
                use(q - 1)
        use(last)

        @pl.when(p < replicas - 1)
        def _():
            down_grad(p)

        for s in range(3):

            @pl.when(p == s)
            def _():
                for side in range(2):
                    if s == 2:
                        dn_copy(0, 1 - side).wait_recv()
                        dn[2, side] = add(dn[2, side], dn_far[1 - side, 0])
                    dn_copy(s, side).start()

        @pl.when(p == 0)
        def _():
            for zp in range(chips):
                remote(
                    part.at[zp * 2 + (1 - c)], sib_part.at[zp], part_sib.at[zp],
                    part_sib_recv.at[zp], "expert", sibling,
                ).wait_recv()
                part[zp * 2 + c] = add(part[zp * 2 + c], sib_part[zp])

        @pl.when(p == replicas - 2)
        def _():
            pl.when(inner)(part_copy(2).start)

    @pl.when(inner)
    def _():
        part_copy(0).start()

    @pl.when(outer)
    def _():
        for m in (1, 2, 3):
            part_copy(m).start()

    def gu_copy(s, side, n):
        to = jnp.where(side == 0, dx, dy)
        return remote(
            gu.at[s, side, n], gu_far.at[side, s, n], gu_send.at[s, side, n],
            gu_recv.at[side, s, n], "dp", to,
        )

    @pl.loop(0, 4 * replicas)
    def _(k):
        s = k // 4
        n = (k // 2) % 2
        side = k % 2
        lhs = rows[:, :, cols_of(s, side)].reshape(experts * count, half)
        gu[s, side, n] = lax.dot_general(
            lhs, back[:, pl.ds(pl.multiple_of(n * ff, ff), ff)], (((0,), (0,)), ((), ())),
            preferred_element_type=f32,
        ).astype(bf16)

        @pl.when(s == 2)
        def _():
            gu_copy(0, 1 - side, n).wait_recv()
            gu[2, side, n] = add(gu[2, side, n], gu_far[1 - side, 0, n])

        @pl.when(s < 3)
        def _():
            gu_copy(s, side, n).start()

    pl.when(inner)(part_copy(3).start)
    down_grad(replicas - 1)

    def total(own, one, two):
        return (own.astype(f32) + one.astype(f32) + two.astype(f32)).astype(bf16)

    def down_store(side):
        return pltpu.make_async_copy(
            dn.at[3, side], down_out.at[:, pl.ds(side * half, half)], out_sem.at[side]
        )

    for side in range(2):
        dn_copy(1, side).wait_recv()
        dn_copy(2, 1 - side).wait_recv()
        dn[3, side] = total(dn[3, side], dn_far[side, 1], dn_far[1 - side, 2])
        down_store(side).start()

    def far_copy(m):
        zp = at_chip(m)
        return remote(
            part.at[zp * 2 + c], far_part.at[zp], part_send.at[m], part_recv.at[zp], "expert",
            zp * 2 + c,
        )

    for m in range(chips):
        pl.when(zm != m)(far_copy(m).wait_recv)
    mixed = part[me].astype(f32)
    for q in range(1, chips):
        mixed = mixed + far_part[source(q)].astype(f32)
    part[me] = mixed.astype(bf16)
    mixed_store = pltpu.make_async_copy(part.at[me], combined, out_sem.at[2])
    mixed_store.start()

    def gu_store(side, n):
        return pltpu.make_async_copy(
            gu.at[3, side, n], (gate_out, up_out)[n].at[pl.ds(side * half, half)],
            out_sem.at[3 + 2 * n + side],
        )

    for n in range(2):
        for side in range(2):
            gu_copy(1, side, n).wait_recv()
            gu_copy(2, 1 - side, n).wait_recv()
            gu[3, side, n] = total(gu[3, side, n], gu_far[side, 1, n], gu_far[1 - side, 2, n])
            gu_store(side, n).start()

    own_to_sib.wait_send()
    for h in range(2):
        tok_own(1, h).wait_send()

        @pl.when(inner)
        def _():
            tok_own(0, h).wait_send()
            tok_hop(1, at_chip(0), h).wait_send()
            tok_hop(0, at_chip(2), h).wait_send()
            tok_hop(0, at_chip(3), h).wait_send()

    for p in range(replicas):
        cot_hop(1, p, z).wait_send()

        @pl.when(inner)
        def _():
            cot_hop(0, p, z).wait_send()
            cot_hop(1, p, at_chip(0)).wait_send()
            cot_hop(0, p, at_chip(2)).wait_send()
            cot_hop(0, p, at_chip(3)).wait_send()

    for r in range(1, experts):
        wt_copy(r).wait_send()
    for q in range(chips):
        zp = source(q)
        if q > 0:
            tok_to_sib(zp).wait_send()
        part_to_sib(zp).wait_send()
        for p in range(replicas):
            cot_to_sib(p, zp).wait_send()
        pl.when(zm != q)(part_copy(q).wait_send)
    for s in range(3):
        for side in range(2):
            dn_copy(s, side).wait_send()
            for n in range(2):
                gu_copy(s, side, n).wait_send()
    for side in range(2):
        down_store(side).wait()
        for n in range(2):
            gu_store(side, n).wait()
    mixed_store.wait()


def chain_local(tokens, expert_ids, probs, trade, gate_weight, up_weight, down_weight, out_grad):
    count, width = tokens.shape
    ff = gate_weight.shape[2]
    experts = lax.axis_size("expert")
    replicas = lax.axis_size("dp")
    chips = experts // 2
    share = width // replicas
    half = share // 2
    halfway = experts // 2
    numbers = jnp.arange(experts, dtype=jnp.int32)
    owners = jnp.where(
        jnp.concatenate([trade, trade]) == 1, jnp.bitwise_xor(numbers, halfway), numbers
    )
    weights = jnp.sum(
        jnp.where(expert_ids.T[None] == owners[:, None, None], probs.T[None], 0.0), axis=1
    )
    bf16, f32 = jnp.bfloat16, jnp.float32
    dma = pltpu.SemaphoreType.DMA
    total = experts * count
    hbm = pl.BlockSpec(memory_space=pl.ANY)
    combined, gate, up, down = pl.pallas_call(
        layer_kernel,
        out_shape=(
            jax.ShapeDtypeStruct((count, width), bf16),
            jax.ShapeDtypeStruct((share, ff), bf16),
            jax.ShapeDtypeStruct((share, ff), bf16),
            jax.ShapeDtypeStruct((ff, share), bf16),
        ),
        in_specs=[hbm] * 6,
        out_specs=(hbm,) * 4,
        scratch_shapes=[
            pltpu.VMEM((experts, count, width), bf16),
            pltpu.VMEM((replicas, experts, count, share), bf16),
            pltpu.VMEM((experts, experts, count), f32),
            pltpu.VMEM((width, ff), bf16),
            pltpu.VMEM((width, ff), bf16),
            pltpu.VMEM((ff, width), bf16),
            pltpu.VMEM((total, count), f32),
            pltpu.VMEM((total, ff), bf16),
            pltpu.VMEM((total, 2 * ff), bf16),
            pltpu.VMEM((total, ff), f32),
            pltpu.VMEM((total, share), bf16),
            pltpu.VMEM((experts, count, width), bf16),
            pltpu.VMEM((chips, count, width), bf16),
            pltpu.VMEM((chips, count, width), bf16),
            pltpu.VMEM((4, 2, 2, half, ff), bf16),
            pltpu.VMEM((2, 3, 2, half, ff), bf16),
            pltpu.VMEM((4, 2, ff, half), bf16),
            pltpu.VMEM((2, 3, ff, half), bf16),
            dma((5 + 2 * replicas,)),
            dma((7,)),
            dma((2, chips, 2)),
            dma((chips,)),
            dma((experts, 2)),
            dma((2, replicas, chips)),
            dma((replicas, chips)),
            dma((replicas, experts)),
            dma((experts,)),
            dma((experts,)),
            dma((chips,)),
            dma((chips,)),
            dma((chips,)),
            dma((chips,)),
            dma((3, 2, 2)),
            dma((2, 3, 2)),
            dma((3, 2)),
            dma((2, 3)),
        ],
        compiler_params=pltpu.CompilerParams(
            collective_id=0, has_side_effects=True, vmem_limit_bytes=67043328
        ),
    )(tokens, out_grad, weights, gate_weight[0], up_weight[0], down_weight[0])
    return combined, gate[None], up[None], down[None]


def local(tokens, expert_ids, *rest):
    experts, replicas = lax.axis_size("expert"), lax.axis_size("dp")
    capacity = 5 * tokens.shape[0] * expert_ids.shape[1] // (4 * experts)
    if tokens.shape[0] <= 2 * capacity and experts == 8 and replicas == 4:
        return chain_local(tokens, expert_ids, *rest)
    return sparse_local(tokens, expert_ids, *rest)


def solution(mesh):
    return jax.shard_map(
        local,
        mesh=mesh,
        in_specs=(
            P(("dp", "expert"), None),
            P(("dp", "expert"), None),
            P(("dp", "expert"), None),
            P(),
            P("expert", None, None),
            P("expert", None, None),
            P("expert", None, None),
            P(("dp", "expert"), None),
        ),
        out_specs=(
            P(("dp", "expert"), None),
            P("expert", "dp", None),
            P("expert", "dp", None),
            P("expert", None, "dp"),
        ),
        check_vma=False,
    )
```

time: 173 us -> 146 us (0.84)
  Pallas kernels: 164 us -> 137 us
    pallas_call x1, Pallas kernels: 164 us -> 137 us  [chain_local(): pl.pallas_call(layer_kernel, out_shape=(jax.ShapeDtypeStruct((count, widt...]
where the time goes in v1:
time: 146 us
  Pallas kernels  137 us (94%)
  local copies, waits for them, and re-layouts  5.83 us (4%)
  other arithmetic  2.17 us (1%)
    pallas_call x1, Pallas kernels, chain_local(): pl.pallas_call(layer_kernel, out_shape=(jax.ShapeDtypeStruct((count, widt...  137 us
    unnamed x8, local copies, waits for them, and re-layouts  5.83 us

profile of v1, /device:TPU:0, one launch (start us, length us, event | category | flops | bytes accessed | tf_op | source)
XLA Modules:
  0.0 145.6 jit_solution(13577322393729844502)
XLA Ops:
  0.6 0.8 compare_select_fusion
  1.4 1.4 select_reduce_fusion.weights
  2.8 137.0 %shard_map.111 = (bf16[128,2048]{1,0:T(8,128)(2,1)}, bf16[512,768]{1,0:T(8,128)(2,1)}, bf16[512,768]{1,0:T(8,128)(2,1)}, bf16[768,512]{1,0:T(8,128)(2,1)}) custom-call(bf16[128,2048]{1,0:T(8,128)(2,1)} %tokens.1, bf16[128,2048]{1,0:T(8,128)(2,1)} %grads.1, f32[8,128]{1,0:T(8,128)} %select_reduce_fusion.weights, bf16[2048,768]{1,0:T(8,128)(2,1)} %bitcast.8, ...), custom_call_target="tpu_custom_call" | custom-call | tf_op jit(solution)/shard_map/pallas_call | solution.py:581
  139.8 0.0 copy-start.1
  139.8 0.0 copy-start
  139.8 2.0 %copy.16 = bf16[128,2048]{1,0:T(8,128)(2,1)} copy(bf16[128,2048]{1,0:T(8,128)(2,1)} %get-tuple-element.16) | data formatting | bytes 1048576
  141.8 2.1 %copy.17 = bf16[1,512,768]{2,1,0:T(8,128)(2,1)} copy(bf16[1,512,768]{2,1,0:T(8,128)(2,1)} %bitcast.13) | data formatting | bytes 1572864
  143.8 0.0 copy-done.1
  143.8 0.9 copy.18
  144.7 0.0 copy-done
  144.7 0.9 copy.19
Async XLA Ops:
  139.8 4.1 %copy-start.1 = (bf16[512,768]{1,0:T(8,128)(2,1)S(1)}, bf16[512,768]{1,0:T(8,128)(2,1)}, u32[]{:S(2)}) copy-start(bf16[512,768]{1,0:T(8,128)(2,1)} %get-tuple-element.10) | copy-start | bytes 2359300
  139.8 5.0 %copy-start = (bf16[768,512]{1,0:T(8,128)(2,1)S(1)}, bf16[768,512]{1,0:T(8,128)(2,1)}, u32[]{:S(2)}) copy-start(bf16[768,512]{1,0:T(8,128)(2,1)} %get-tuple-element.11) | copy-start | bytes 2359300

commit v2 on v1

--- a/solution.py
+++ b/solution.py
@@ -93,8 +93,9 @@
 
 
 def layer_kernel(
-    tokens, grads, weights, wg_hbm, wu_hbm, wd_hbm, combined, gate_out, up_out, down_out,
-    rows, cots, wts, wg, wu, wd, wcol, hidden, back, acc, pairs, part, sib_part, far_part,
+    tokens, grads, ids, probs, trade, wg_hbm, wu_hbm, wd_hbm,
+    combined, gate_out, up_out, down_out,
+    rows, cots, all_ids, all_probs, wg, wu, wd, wcol, hidden, back, acc, pairs, part, sib_part, far_part,
     gu, gu_far, dn, dn_far,
     load_sem, out_sem, tok_send, tok_sib, tok_recv, cot_send, cot_sib, cot_recv, wt_send, wt_recv,
     part_sib, part_sib_recv, part_send, part_recv, gu_send, gu_recv, dn_send, dn_recv,
@@ -146,17 +147,18 @@
         pltpu.make_async_copy(wu_hbm, wu, load_sem.at[1]),
         pltpu.make_async_copy(wd_hbm, wd, load_sem.at[2]),
         pltpu.make_async_copy(tokens, rows.at[me], load_sem.at[3]),
-        pltpu.make_async_copy(weights, wts.at[me], load_sem.at[4]),
+        pltpu.make_async_copy(ids, all_ids.at[me], load_sem.at[4]),
+        pltpu.make_async_copy(probs, all_probs.at[me], load_sem.at[5]),
     ]
 
     def cot_load(p, side):
         return pltpu.make_async_copy(
             grads.at[:, cols_of(p, side)], cots.at[p, me, :, pl.ds(side * half, half)],
-            load_sem.at[5 + 2 * p + side],
-        )
-
-    loads[3].start()
-    loads[4].start()
+            load_sem.at[6 + 2 * p + side],
+        )
+
+    for load in loads[3:]:
+        load.start()
     for p in range(replicas):
         for side in range(2):
             cot_load(p, side).start()
@@ -205,14 +207,16 @@
         ref = cots.at[p, zp * 2 + c]
         return remote(ref, ref, cot_sib.at[p, zp], cot_recv.at[p, zp * 2 + c], "expert", sibling)
 
-    def wt_copy(r):
-        return remote(
-            weights, wts.at[me], wt_send.at[r], wt_recv.at[me], "expert", (me + r) % experts
-        )
-
-    def wt_from(slot):
-        return remote(
-            weights, wts.at[slot], wt_send.at[1], wt_recv.at[slot], "expert", sibling
+    def route_copy(r, k):
+        ref, dst = ((ids, all_ids), (probs, all_probs))[k]
+        return remote(
+            ref, dst.at[me], wt_send.at[k, r], wt_recv.at[k, me], "expert", (me + r) % experts
+        )
+
+    def route_from(slot, k):
+        ref, dst = ((ids, all_ids), (probs, all_probs))[k]
+        return remote(
+            ref, dst.at[slot], wt_send.at[k, 1], wt_recv.at[k, slot], "expert", sibling
         )
 
     own_to_sib = remote(
@@ -220,7 +224,8 @@
     )
 
     for r in range(1, experts):
-        wt_copy(r).start()
+        for k in range(2):
+            route_copy(r, k).start()
     own_to_sib.start()
     for h in range(2):
         tok_own(1, h).start()
@@ -242,15 +247,22 @@
         jnp.int32, (count, count), 1
     )
 
+    halfway = experts // 2
+    swapped = jnp.where(me < halfway, me + halfway, me - halfway)
+    name = jnp.where(trade[me % halfway] == 1, swapped, me)
+
     def weight_column(slot):
-        row = jnp.broadcast_to(wts[slot, pl.ds(me, 1), :], (count, count))
+        row = jnp.sum(
+            jnp.where(all_ids[slot] == name, all_probs[slot], 0.0), axis=0, keepdims=True
+        )
+        row = jnp.broadcast_to(row, (count, count))
         column = jnp.sum(jnp.where(eye, row, 0.0), axis=1, keepdims=True)
         wcol[pl.ds(pl.multiple_of(slot * count, count), count), :] = jnp.broadcast_to(
             column, (count, wcol.shape[1])
         )
 
-    loads[3].wait()
-    loads[4].wait()
+    for load in loads[3:]:
+        load.wait()
 
     @pl.loop(0, chips)
     def _(q):
@@ -296,7 +308,8 @@
 
         @pl.when(q == 0)
         def _():
-            wt_from(sibling).wait_recv()
+            for k in range(2):
+                route_from(sibling, k).wait_recv()
             weight_column(me)
             weight_column(sibling)
             for load in loads[:3]:
@@ -305,7 +318,8 @@
         @pl.when(q > 0)
         def _():
             for k in range(2):
-                wt_from(zp * 2 + k).wait_recv()
+                for part_of in range(2):
+                    route_from(zp * 2 + k, part_of).wait_recv()
                 weight_column(zp * 2 + k)
 
         remote(
@@ -429,18 +443,18 @@
                 ).wait_recv()
                 part[zp * 2 + c] = add(part[zp * 2 + c], sib_part[zp])
 
-        @pl.when(p == replicas - 2)
-        def _():
-            pl.when(inner)(part_copy(2).start)
+        @pl.when(jnp.logical_and(outer, p == 1))
+        def _():
+            part_copy(1).start()
+            part_copy(2).start()
+
+        pl.when(jnp.logical_and(inner, p == replicas - 2))(part_copy(2).start)
 
     @pl.when(inner)
     def _():
         part_copy(0).start()
 
-    @pl.when(outer)
-    def _():
-        for m in (1, 2, 3):
-            part_copy(m).start()
+    pl.when(outer)(part_copy(3).start)
 
     def gu_copy(s, side, n):
         to = jnp.where(side == 0, dx, dy)
@@ -537,7 +551,8 @@
             cot_hop(0, p, at_chip(3)).wait_send()
 
     for r in range(1, experts):
-        wt_copy(r).wait_send()
+        for k in range(2):
+            route_copy(r, k).wait_send()
     for q in range(chips):
         zp = source(q)
         if q > 0:
@@ -558,6 +573,19 @@
     mixed_store.wait()
 
 
+def hand_on(*refs):
+    arrays, outs, held, sems = refs[:4], refs[4:8], refs[8:12], refs[12]
+    into = [pltpu.make_async_copy(arrays[k], held[k], sems.at[0, k]) for k in range(4)]
+    back = [pltpu.make_async_copy(held[k], outs[k], sems.at[1, k]) for k in range(4)]
+    for copy in into:
+        copy.start()
+    for k in range(4):
+        into[k].wait()
+        back[k].start()
+    for copy in back:
+        copy.wait()
+
+
 def chain_local(tokens, expert_ids, probs, trade, gate_weight, up_weight, down_weight, out_grad):
     count, width = tokens.shape
     ff = gate_weight.shape[2]
@@ -566,19 +594,12 @@
     chips = experts // 2
     share = width // replicas
     half = share // 2
-    halfway = experts // 2
-    numbers = jnp.arange(experts, dtype=jnp.int32)
-    owners = jnp.where(
-        jnp.concatenate([trade, trade]) == 1, jnp.bitwise_xor(numbers, halfway), numbers
-    )
-    weights = jnp.sum(
-        jnp.where(expert_ids.T[None] == owners[:, None, None], probs.T[None], 0.0), axis=1
-    )
+    top = expert_ids.shape[1]
     bf16, f32 = jnp.bfloat16, jnp.float32
     dma = pltpu.SemaphoreType.DMA
     total = experts * count
     hbm = pl.BlockSpec(memory_space=pl.ANY)
-    combined, gate, up, down = pl.pallas_call(
+    results = pl.pallas_call(
         layer_kernel,
         out_shape=(
             jax.ShapeDtypeStruct((count, width), bf16),
@@ -586,12 +607,13 @@
             jax.ShapeDtypeStruct((share, ff), bf16),
             jax.ShapeDtypeStruct((ff, share), bf16),
         ),
-        in_specs=[hbm] * 6,
+        in_specs=[hbm] * 4 + [pl.BlockSpec(memory_space=pltpu.SMEM)] + [hbm] * 3,
         out_specs=(hbm,) * 4,
         scratch_shapes=[
             pltpu.VMEM((experts, count, width), bf16),
             pltpu.VMEM((replicas, experts, count, share), bf16),
-            pltpu.VMEM((experts, experts, count), f32),
+            pltpu.VMEM((experts, top, count), jnp.int32),
+            pltpu.VMEM((experts, top, count), f32),
             pltpu.VMEM((width, ff), bf16),
             pltpu.VMEM((width, ff), bf16),
             pltpu.VMEM((ff, width), bf16),
@@ -607,7 +629,7 @@
             pltpu.VMEM((2, 3, 2, half, ff), bf16),
             pltpu.VMEM((4, 2, ff, half), bf16),
             pltpu.VMEM((2, 3, ff, half), bf16),
-            dma((5 + 2 * replicas,)),
+            dma((6 + 2 * replicas,)),
             dma((7,)),
             dma((2, chips, 2)),
             dma((chips,)),
@@ -615,8 +637,8 @@
             dma((2, replicas, chips)),
             dma((replicas, chips)),
             dma((replicas, experts)),
-            dma((experts,)),
-            dma((experts,)),
+            dma((2, experts)),
+            dma((2, experts)),
             dma((chips,)),
             dma((chips,)),
             dma((chips,)),
@@ -629,7 +651,17 @@
         compiler_params=pltpu.CompilerParams(
             collective_id=0, has_side_effects=True, vmem_limit_bytes=67043328
         ),
-    )(tokens, out_grad, weights, gate_weight[0], up_weight[0], down_weight[0])
+    )(
+        tokens, out_grad, expert_ids.T, probs.T, trade,
+        gate_weight[0], up_weight[0], down_weight[0],
+    )
+    combined, gate, up, down = pl.pallas_call(
+        hand_on,
+        out_shape=[jax.ShapeDtypeStruct(r.shape, r.dtype) for r in results],
+        in_specs=[hbm] * 4,
+        out_specs=[hbm] * 4,
+        scratch_shapes=[pltpu.VMEM(r.shape, r.dtype) for r in results] + [dma((2, 4))],
+    )(*results)
     return combined, gate[None], up[None], down[None]
 
 

time: 146 us -> 141 us (0.966)
  local copies, waits for them, and re-layouts: 5.83 us -> 0 us
  Pallas kernels: 137 us -> 141 us
  other arithmetic: 2.17 us -> 0 us
    unnamed x8 -> x0, local copies, waits for them, and re-layouts: 5.83 us -> none
    pallas_call x0 -> x1, Pallas kernels: none -> 2.76 us  [chain_local(): pl.pallas_call(hand_on, out_shape=[jax.ShapeDtypeStruct(r.shape, r.dtype)...]
where the time goes in v2:
time: 141 us
  Pallas kernels  141 us (100%)
    pallas_call x1, Pallas kernels, chain_local(): pl.pallas_call(layer_kernel, out_shape=(jax.ShapeDtypeStruct((count, widt...  138 us

profile of v2, /device:TPU:0, one launch (start us, length us, event | category | flops | bytes accessed | tf_op | source)
XLA Modules:
  0.0 141.3 jit_solution(7567239786197845681)
XLA Ops:
  0.6 137.9 %shard_map.111 = (bf16[128,2048]{1,0:T(8,128)(2,1)}, bf16[512,768]{1,0:T(8,128)(2,1)}, bf16[512,768]{1,0:T(8,128)(2,1)}, bf16[768,512]{1,0:T(8,128)(2,1)}) custom-call(bf16[128,2048]{1,0:T(8,128)(2,1)} %tokens.1, bf16[128,2048]{1,0:T(8,128)(2,1)} %grads.1, s32[4,128]{1,0:T(4,128)} %bitcast.11, f32[4,128]{1,0:T(4,128)} %bitcast.12, s32[4]{0:T(128)} %trade.1, ...), custom_call_target="tpu_custom_call" | custom-call | tf_op jit(solution)/shard_map/pallas_call | solution.py:602
  138.5 2.8 %shard_map.112 = (bf16[128,2048]{1,0:T(8,128)(2,1)}, bf16[512,768]{1,0:T(8,128)(2,1)}, bf16[512,768]{1,0:T(8,128)(2,1)}, bf16[768,512]{1,0:T(8,128)(2,1)}) custom-call(bf16[128,2048]{1,0:T(8,128)(2,1)} %get-tuple-element.12.refs_0_, bf16[512,768]{1,0:T(8,128)(2,1)} %get-tuple-element.13.refs_1_, bf16[512,768]{1,0:T(8,128)(2,1)} %get-tuple-element.14.refs_2_, ...), custom_call_target="tpu_custom_call" | custom-call | tf_op jit(solution)/shard_map/pallas_call | solution.py:658

commit v3 on v2

--- a/solution.py
+++ b/solution.py
@@ -96,9 +96,10 @@
     tokens, grads, ids, probs, trade, wg_hbm, wu_hbm, wd_hbm,
     combined, gate_out, up_out, down_out,
     rows, cots, all_ids, all_probs, wg, wu, wd, wcol, hidden, back, acc, pairs, part, sib_part, far_part,
-    gu, gu_far, dn, dn_far,
+    gu, gu_far, dn, dn_far, via,
     load_sem, out_sem, tok_send, tok_sib, tok_recv, cot_send, cot_sib, cot_recv, wt_send, wt_recv,
     part_sib, part_sib_recv, part_send, part_recv, gu_send, gu_recv, dn_send, dn_recv,
+    via_send, via_recv, rest_send, rest_recv,
 ):
     f32 = jnp.float32
     bf16 = jnp.bfloat16
@@ -137,9 +138,10 @@
         return pl.ds(pl.multiple_of(owner * share + h * half, half), half)
 
     def remote(src, dst, ssem, rsem, axis, to):
+        device = to if axis is None else {axis: to}
         return pltpu.make_async_remote_copy(
             src_ref=src, dst_ref=dst, send_sem=ssem, recv_sem=rsem,
-            device_id={axis: to}, device_id_type=pl.DeviceIdType.MESH,
+            device_id=device, device_id_type=pl.DeviceIdType.MESH,
         )
 
     loads = [
@@ -175,7 +177,11 @@
         pl.semaphore_signal(
             barrier, inc=1, device_id={"dp": to}, device_id_type=pl.DeviceIdType.MESH
         )
-    pl.semaphore_wait(barrier, experts + 1)
+        pl.semaphore_signal(
+            barrier, inc=1, device_id={"dp": to, "expert": at_chip(1 - zm) * 2 + c},
+            device_id_type=pl.DeviceIdType.MESH,
+        )
+    pl.semaphore_wait(barrier, experts + 3)
 
     to_chip = (at_chip(0) * 2 + c, at_chip(zm + 1) * 2 + c)
     rhalf = count // 2
@@ -450,18 +456,44 @@
 
         pl.when(jnp.logical_and(inner, p == replicas - 2))(part_copy(2).start)
 
-    @pl.when(inner)
-    def _():
-        part_copy(0).start()
-
-    pl.when(outer)(part_copy(3).start)
-
-    def gu_copy(s, side, n):
+    pl.when(inner)(part_copy(0).start)
+
+    detour = via.shape[1]
+    rest = pl.ds(half - detour, detour)
+
+    def gu_copy(s, side, n, short=False):
         to = jnp.where(side == 0, dx, dy)
+        if short:
+            kept = pl.ds(0, half - detour)
+            return remote(
+                gu.at[s, side, n, kept], gu_far.at[side, s, n, kept], gu_send.at[s, side, n],
+                gu_recv.at[side, s, n], "dp", to,
+            )
         return remote(
             gu.at[s, side, n], gu_far.at[side, s, n], gu_send.at[s, side, n],
             gu_recv.at[side, s, n], "dp", to,
         )
+
+    def rest_copy(side):
+        return remote(
+            gu.at[1, side, 1, rest], gu_far.at[side, 1, 1, rest], rest_send.at[side],
+            rest_recv.at[side], "dp", jnp.where(side == 0, dx, dy),
+        )
+
+    def via_copy(side):
+        to = jnp.where(side == 0, dx, dy)
+        return remote(
+            gu.at[1, side, 1, rest], via.at[side], rest_send.at[side], via_recv.at[side], None,
+            {"dp": to, "expert": at_chip(1) * 2 + c},
+        )
+
+    def via_hop(side):
+        return remote(
+            via.at[side], gu_far.at[side, 1, 1, rest], via_send.at[side], rest_recv.at[side],
+            "expert", at_chip(0) * 2 + c,
+        )
+
+    pl.when(outer)(part_copy(3).start)
 
     @pl.loop(0, 4 * replicas)
     def _(k):
@@ -479,12 +511,26 @@
             gu_copy(0, 1 - side, n).wait_recv()
             gu[2, side, n] = add(gu[2, side, n], gu_far[1 - side, 0, n])
 
-        @pl.when(s < 3)
+        apart = jnp.logical_and(s == 1, n == 1)
+
+        @pl.when(jnp.logical_and(s < 3, jnp.logical_not(apart)))
         def _():
             gu_copy(s, side, n).start()
+
+        @pl.when(apart)
+        def _():
+            pl.when(outer)(via_copy(side).start)
+            gu_copy(1, side, 1, True).start()
+            pl.when(inner)(rest_copy(side).start)
 
     pl.when(inner)(part_copy(3).start)
     down_grad(replicas - 1)
+
+    @pl.when(inner)
+    def _():
+        for side in range(2):
+            via_copy(side).wait_recv()
+            via_hop(side).start()
 
     def total(own, one, two):
         return (own.astype(f32) + one.astype(f32) + two.astype(f32)).astype(bf16)
@@ -524,7 +570,9 @@
 
     for n in range(2):
         for side in range(2):
-            gu_copy(1, side, n).wait_recv()
+            gu_copy(1, side, n, n == 1).wait_recv()
+            if n == 1:
+                rest_copy(side).wait_recv()
             gu_copy(2, 1 - side, n).wait_recv()
             gu[3, side, n] = total(gu[3, side, n], gu_far[side, 1, n], gu_far[1 - side, 2, n])
             gu_store(side, n).start()
@@ -565,7 +613,10 @@
         for side in range(2):
             dn_copy(s, side).wait_send()
             for n in range(2):
-                gu_copy(s, side, n).wait_send()
+                gu_copy(s, side, n, (s, n) == (1, 1)).wait_send()
+        if s < 2:
+            pl.when(inner)(via_hop(s).wait_send)
+            rest_copy(s).wait_send()
     for side in range(2):
         down_store(side).wait()
         for n in range(2):
@@ -629,6 +680,7 @@
             pltpu.VMEM((2, 3, 2, half, ff), bf16),
             pltpu.VMEM((4, 2, ff, half), bf16),
             pltpu.VMEM((2, 3, ff, half), bf16),
+            pltpu.VMEM((2, half // 2, ff), bf16),
             dma((6 + 2 * replicas,)),
             dma((7,)),
             dma((2, chips, 2)),
@@ -647,6 +699,10 @@
             dma((2, 3, 2)),
             dma((3, 2)),
             dma((2, 3)),
+            dma((2,)),
+            dma((2,)),
+            dma((2,)),
+            dma((2,)),
         ],
         compiler_params=pltpu.CompilerParams(
             collective_id=0, has_side_effects=True, vmem_limit_bytes=67043328

time: 141 us -> 137 us (0.972)
  Pallas kernels: 141 us -> 137 us
    pallas_call x1, Pallas kernels: 138 us -> 134 us  [chain_local(): pl.pallas_call(layer_kernel, out_shape=(jax.ShapeDtypeStruct((count, widt...]
where the time goes in v3:
time: 137 us
  Pallas kernels  137 us (100%)
    pallas_call x1, Pallas kernels, chain_local(): pl.pallas_call(layer_kernel, out_shape=(jax.ShapeDtypeStruct((count, widt...  134 us
    pallas_call x1, Pallas kernels, chain_local(): pl.pallas_call(hand_on, out_shape=[jax.ShapeDtypeStruct(r.shape, r.dtype)...  2.76 us

profile of v3, /device:TPU:0, one launch (start us, length us, event | category | flops | bytes accessed | tf_op | source)
XLA Modules:
  0.0 137.2 jit_solution(503882106915836697)
XLA Ops:
  0.6 133.8 %shard_map.111 = (bf16[128,2048]{1,0:T(8,128)(2,1)}, bf16[512,768]{1,0:T(8,128)(2,1)}, bf16[512,768]{1,0:T(8,128)(2,1)}, bf16[768,512]{1,0:T(8,128)(2,1)}) custom-call(bf16[128,2048]{1,0:T(8,128)(2,1)} %tokens.1, bf16[128,2048]{1,0:T(8,128)(2,1)} %grads.1, s32[4,128]{1,0:T(4,128)} %bitcast.11, f32[4,128]{1,0:T(4,128)} %bitcast.12, s32[4]{0:T(128)} %trade.1, ...), custom_call_target="tpu_custom_call" | custom-call | tf_op jit(solution)/shard_map/pallas_call | solution.py:653
  134.4 2.8 %shard_map.112 = (bf16[128,2048]{1,0:T(8,128)(2,1)}, bf16[512,768]{1,0:T(8,128)(2,1)}, bf16[512,768]{1,0:T(8,128)(2,1)}, bf16[768,512]{1,0:T(8,128)(2,1)}) custom-call(bf16[128,2048]{1,0:T(8,128)(2,1)} %get-tuple-element.12.refs_0_, bf16[512,768]{1,0:T(8,128)(2,1)} %get-tuple-element.13.refs_1_, bf16[512,768]{1,0:T(8,128)(2,1)} %get-tuple-element.14.refs_2_, ...), custom_call_target="tpu_custom_call" | custom-call | tf_op jit(solution)/shard_map/pallas_call | solution.py:714
